TPU v7x, 128 devices: a whole 4x4x4 slice. The times are simulated.
128 devices in a mesh: seq: 32 (over x_hi, z, y), tensor: 2 (over core), dp: 2 (over x_lo).
Axes of the slice: x: 4 (x_hi: 2, x_lo: 2; x = x_hi * 2 + x_lo), y: 4, z: 4, core: 2. Of those that a mesh axis runs over, the one named last changes fastest.
Arguments:
- inputs: bfloat16 [2, 24576, 1536], P('dp', 'seq', 'tensor'), may hold values from -6 to 6
- lengths: int32 [2], P('dp'), may hold values from 6144 to 24576, as said below
- cotangent: bfloat16 [2, 24576, 1536], P('dp', 'seq', 'tensor'), may hold values from -6 to 6
- w_value: bfloat16 [1536, 1536], P(None, 'tensor'), may hold values from -0.15625 to 0.15625
- w_gate: bfloat16 [1536, 1536], P(None, 'tensor'), may hold values from -0.15625 to 0.15625
- kernel: bfloat16 [31, 1536], P(None, 'tensor'), may hold values from -1 to 1
- w_out: bfloat16 [1536, 1536], P('tensor'), may hold values from -0.15625 to 0.15625
Outputs:
- output: bfloat16 [2, 24576, 1536], P('dp', 'seq', 'tensor')
- input_gradient: bfloat16 [2, 24576, 1536], P('dp', 'seq', 'tensor')
- value_grad: float32 [1536, 1536], P(('seq', 'dp'), 'tensor')
- gate_grad: float32 [1536, 1536], P(('seq', 'dp'), 'tensor')
- kernel_grad: float32 [31, 1536], P(None, 'tensor')
- out_grad: float32 [1536, 1536], P('tensor', ('seq', 'dp'))
Inputs may be any that keep to these rules, and one draw needn't show every extreme that they name: `lengths`: in every draw some utterance has all 24576 frames valid.
All inputs are finite; a program needn't handle non-finite values.
Results may differ from a plain program's by a relative error of at most 0.009.
Values may be sent and summed in bfloat16 or wider, within the bound.
A program may use at most 128 MiB of HBM per device.

v0:
```python
import functools

import jax
import jax.numpy as jnp
from jax import lax
from jax.experimental import pallas as pl
from jax.experimental.pallas import tpu as pltpu
from jax.sharding import PartitionSpec as P

epsilon = 1e-05
MESH = pl.DeviceIdType.MESH
BF16, F32 = jnp.bfloat16, jnp.float32
ORDERS = ("xyz", "yzx", "zxy")
GRADS = 3
FRAMES, WIDTH, HALF = 768, 1536, 768
ROWS, CHUNKS = 256, 3
GROUP = 16
SPREAD = ROWS // 8
TAPS, REACH, EDGE = 31, 15, 16
LEFT = {
    "xyz": ((4, 4), (4,), ()),
    "yzx": ((2, 4, 2), (2, 2), ()),
    "zxy": ((2, 4, 2), (4,), ()),
}


class Torus:
    def __init__(self):
        seq, low = lax.axis_index("seq"), lax.axis_index("dp")
        self.at = {
            "x": lax.div(seq, 16) * 2 + low,
            "y": lax.rem(seq, 4),
            "z": lax.rem(lax.div(seq, 4), 4),
        }

    def moved(self, axis, by):
        return lax.rem(self.at[axis] + (by + 4), 4)

    def beside(self, by):
        return {"seq": lax.rem(lax.axis_index("seq") + (by + 32), 32)}

    def peer(self, axis, by):
        at = dict(self.at)
        at[axis] = self.moved(axis, by)
        return {
            "seq": (lax.div(at["x"], 2) * 4 + at["z"]) * 4 + at["y"],
            "dp": lax.rem(at["x"], 2),
        }


def part_of(order, phase, coord):
    every = slice(None)
    high, low = lax.div(coord, 2), lax.rem(coord, 2)
    if phase == 0:
        return {
            "x": (high, every, every, low),
            "y": (every, every, coord, every),
            "z": (every, coord, every, every),
        }[order[0]]
    if phase == 1:
        return {"xyz": (every, coord), "yzx": (every, coord, every), "zxy": (high, every, low)}[order]
    return {"xyz": (coord,), "yzx": (high, low), "zxy": (coord,)}[order]


class Scatter:
    def __init__(self, torus, grad, strip, source, landed, sums, out, send, recv):
        self.torus, self.grad, self.strip = torus, grad, strip
        self.source, self.landed, self.sums, self.out = source, landed, sums, out
        self.send, self.recv = send, recv
        self.order = ORDERS[strip // 2]
        self.way = 1 if strip % 2 == 0 else -1

    def held(self, phase, coord):
        part = part_of(self.order, phase, coord)
        if phase == 0:
            return self.source.at[(self.grad, self.strip) + part]
        return self.sums[self.strip // 2][phase - 1].at[(self.grad, self.strip % 2) + part]

    def slot(self, phase, which):
        return self.landed[self.strip // 2][phase].at[self.grad, self.strip % 2, which]

    def copy(self, phase, which, ref, by):
        number = ((self.grad * 6 + self.strip) * 3 + phase) * 3 + which
        return pltpu.make_async_remote_copy(
            src_ref=ref,
            dst_ref=self.slot(phase, which),
            send_sem=self.send.at[number],
            recv_sem=self.recv.at[number],
            device_id=self.torus.peer(self.order[phase], by),
            device_id_type=MESH,
        )

    def place(self, phase, by):
        return self.torus.moved(self.order[phase], by)

    def through(self, phase):
        return self.copy(phase, 0, self.held(phase, self.place(phase, 2)), self.way)

    def straight(self, phase):
        return self.copy(phase, 1, self.held(phase, self.place(phase, -self.way)), -self.way)

    def onward(self, phase):
        return self.copy(phase, 2, self.slot(phase, 0), self.way)

    def begin(self, phase):
        self.through(phase).start()
        self.straight(phase).start()

    def relay(self, phase):
        self.through(phase).wait_recv()
        slot = self.slot(phase, 0)
        mine = self.held(phase, self.place(phase, self.way))
        slot[...] = (slot[...].astype(F32) + mine[...].astype(F32)).astype(BF16)
        self.onward(phase).start()

    def finish(self, phase):
        self.straight(phase).wait_recv()
        self.onward(phase).wait_recv()
        mine = self.held(phase, self.torus.at[self.order[phase]])
        total = (
            mine[...].astype(F32)
            + self.slot(phase, 1)[...].astype(F32)
            + self.slot(phase, 2)[...].astype(F32)
        )
        if phase < 2:
            self.sums[self.strip // 2][phase][self.grad, self.strip % 2] = total.astype(BF16)
        else:
            self.out[self.grad][:, 128 * self.strip : 128 * self.strip + 128] = total

    def drain(self):
        for phase in range(3):
            for copy in (self.through, self.straight, self.onward):
                copy(phase).wait_send()


class TapSum:
    def __init__(self, torus, color, slots, send, recv):
        self.torus, self.color, self.slots, self.send, self.recv = torus, color, slots, send, recv
        self.order = ORDERS[color]

    def copies(self, phase):
        axis = self.order[phase]
        here = self.slots.at[self.color, phase, self.torus.at[axis]]
        base = (self.color * 3 + phase) * 3
        return [
            pltpu.make_async_remote_copy(
                src_ref=here,
                dst_ref=here,
                send_sem=self.send.at[base + by - 1],
                recv_sem=self.recv.at[base + by - 1],
                device_id=self.torus.peer(axis, by),
                device_id_type=MESH,
            )
            for by in (1, 2, 3)
        ]

    def begin(self, phase, value):
        self.slots[self.color, phase, self.torus.at[self.order[phase]]] = value
        for copy in self.copies(phase):
            copy.start()

    def finish(self, phase):
        for copy in self.copies(phase):
            copy.wait_recv()
        slots = self.slots
        total = slots[self.color, phase, 0]
        for place in (1, 2, 3):
            total = total + slots[self.color, phase, place]
        return total

    def drain(self):
        for phase in range(3):
            for copy in self.copies(phase):
                copy.wait_send()


def greet(torus):
    barrier = pltpu.get_barrier_semaphore()
    peers = [torus.peer(axis, by) for axis in "xyz" for by in (1, 2, 3)]
    peers += [torus.beside(1), torus.beside(-1), {"tensor": 1 - lax.axis_index("tensor")}]
    for peer in peers:
        pl.semaphore_signal(barrier, inc=1, device_id=peer, device_id_type=MESH)
    pl.semaphore_wait(barrier, len(peers))


def sigmoid(values):
    return 0.5 * jnp.tanh(0.5 * values) + 0.5


def dot(a, b, contract):
    return lax.dot_general(a, b, (contract, ((), ())), preferred_element_type=F32)


def kernel(lengths, x, cot, w_value, w_gate, taps, w_out, out, grad_in, value_grad, gate_grad, taps_grad, out_grad, *scratch):
    landed = [scratch[3 * c : 3 * c + 3] for c in range(3)]
    sums = [scratch[9 + 2 * c : 11 + 2 * c] for c in range(3)]
    (
        slots, send, recv, tap_send, tap_recv,
        grads, xf, uf, wv, wg, wo, nb, rstd1, vb, sg, hb, db, cb, sw, ds, rstd2, stat_out, stat_in,
        dv, dg, po, part_out, part_in, tap_wide, tap_acc,
        load_sem, x_send, x_recv, u_send, u_recv, halo_send, halo_recv, stat_send, stat_recv, part_send, part_recv, store_sem,
    ) = scratch[15:]
    torus = Torus()
    me = lax.axis_index("tensor")
    other = 1 - me
    partner = {"tensor": other}
    seq = lax.axis_index("seq")

    def remote(src, dst, send_sem, recv_sem, to):
        return pltpu.make_async_remote_copy(
            src_ref=src, dst_ref=dst, send_sem=send_sem, recv_sem=recv_sem, device_id=to, device_id_type=MESH
        )

    def chunk(c):
        return pl.ds(ROWS * c, ROWS)

    def x_load(c):
        return pltpu.make_async_copy(x.at[chunk(c)], xf.at[me, chunk(c)], load_sem.at[c])

    def x_share(c):
        return remote(x.at[chunk(c)], xf.at[me, chunk(c)], x_send.at[c], x_recv.at[c], partner)

    u_load = pltpu.make_async_copy(cot, uf.at[me], load_sem.at[3])
    u_share = remote(cot, uf.at[me], u_send, u_recv, partner)
    wv_load = pltpu.make_async_copy(w_value, wv, load_sem.at[4])
    wg_load = pltpu.make_async_copy(w_gate, wg, load_sem.at[5])
    wo_loads = [
        pltpu.make_async_copy(w_out.at[:, pl.ds(HALF * h, HALF)], wo.at[h], load_sem.at[6 + h])
        for h in range(2)
    ]
    for c in range(CHUNKS):
        x_load(c).start()
    wv_load.start()
    wg_load.start()
    u_load.start()
    for load in wo_loads:
        load.start()
    greet(torus)
    for c in range(CHUNKS):
        x_share(c).start()
    u_share.start()

    tap_rows = taps[...].astype(F32)
    for j in range(6):
        for k in range(TAPS):
            tap_wide[j, k] = jnp.broadcast_to(tap_rows[k : k + 1, 128 * j : 128 * j + 128], (8, 128))

    for c in range(CHUNKS):
        x_load(c).wait()
        x_share(c).wait_recv()

        def normalize(i, _, c=c):
            rows = pl.ds(pl.multiple_of(ROWS * c + GROUP * i, GROUP), GROUP)
            a, b = xf[0, rows, :].astype(F32), xf[1, rows, :].astype(F32)
            mean = (jnp.sum(a, -1, keepdims=True) + jnp.sum(b, -1, keepdims=True)) / WIDTH
            a, b = a - mean, b - mean
            var = (jnp.sum(a * a, -1, keepdims=True) + jnp.sum(b * b, -1, keepdims=True)) / WIDTH
            scale = lax.rsqrt(var + epsilon)
            nb[rows, 0:HALF] = (a * scale).astype(BF16)
            nb[rows, HALF:WIDTH] = (b * scale).astype(BF16)
            rstd1[rows, :] = jnp.broadcast_to(scale, (GROUP, 128))
            return 0

        lax.fori_loop(0, ROWS // GROUP, normalize, 0, unroll=2)

    wv_load.wait()
    wg_load.wait()
    length = lengths[0]

    def valid_rows(first, count):
        position = lax.broadcasted_iota(jnp.int32, (count, 128), 0) + (seq * FRAMES + first)
        return jnp.where(position < length, 1.0, 0.0)

    def gate(c):
        for n in range(3):
            columns = slice(256 * n, 256 * n + 256)
            values = jnp.dot(nb[chunk(c), :], wv[:, columns], preferred_element_type=F32)
            sigma = sigmoid(jnp.dot(nb[chunk(c), :], wg[:, columns], preferred_element_type=F32))
            valid = valid_rows(ROWS * c, ROWS)
            vb[chunk(c), columns] = values
            sg[chunk(c), columns] = sigma
            for half in range(2):
                strip = slice(128 * half, 128 * half + 128)
                hidden = values[:, strip] * sigma[:, strip] * valid
                hb[2 * n + half, pl.ds(EDGE + ROWS * c, ROWS), :] = hidden.astype(BF16).astype(F32)

    def halo(buf, number):
        first, last = pl.ds(EDGE, EDGE), pl.ds(FRAMES, EDGE)
        before, after = pl.ds(0, EDGE), pl.ds(FRAMES + EDGE, EDGE)
        return (
            remote(buf.at[:, first], buf.at[:, after], halo_send.at[number], halo_recv.at[number], torus.beside(-1)),
            remote(buf.at[:, last], buf.at[:, before], halo_send.at[number + 1], halo_recv.at[number + 1], torus.beside(1)),
        )

    def halo_end(copies, buf):
        inside = (
            jnp.where(seq < 31, 1.0, 0.0).astype(F32),
            jnp.where(seq > 0, 1.0, 0.0).astype(F32),
        )
        for copy, keep, rows in zip(copies, inside, (pl.ds(FRAMES + EDGE, EDGE), pl.ds(0, EDGE))):
            copy.wait_recv()
            buf[:, rows, :] = buf[:, rows, :] * keep

    gate(0)
    gate(2)
    h_halo = halo(hb, 0)
    for copy in h_halo:
        copy.start()
    gate(1)

    u_load.wait()
    u_share.wait_recv()
    for load in wo_loads:
        load.wait()
    for c in range(CHUNKS):
        for n in range(3):
            ds[chunk(c), 256 * n : 256 * n + 256] = dot(
                uf[0, chunk(c), :], wo[0, 256 * n : 256 * n + 256, :], ((1,), (1,))
            ) + dot(uf[1, chunk(c), :], wo[1, 256 * n : 256 * n + 256, :], ((1,), (1,)))

    def spread(buf, j, c, r):
        return buf[j, pl.ds(EDGE + ROWS * c + r, 8, stride=SPREAD), :]

    def convolve(buf, c, tap_at):
        def strip(j, _):
            for block in range(SPREAD // 8):
                totals = [None] * 8
                for m in range(8 + TAPS - 1):
                    shifted = spread(buf, j, c, 8 * block + m - REACH)
                    for i in range(max(0, m - TAPS + 1), min(8, m + 1)):
                        term = shifted * tap_wide[j, tap_at(m - i)]
                        totals[i] = term if totals[i] is None else totals[i] + term
                for i in range(8):
                    cb[j, pl.ds(ROWS * c + 8 * block + i, 8, stride=SPREAD), :] = totals[i]
            return 0

        lax.fori_loop(0, 6, strip, 0)

    lane = lax.broadcasted_iota(jnp.int32, (GROUP, 128), 1)

    def stat_copy(number, c):
        at = 3 * number + c
        return remote(
            stat_out.at[number, chunk(c)], stat_in.at[number, chunk(c)], stat_send.at[at], stat_recv.at[at], partner
        )

    def put_stats(number, rows, first, second):
        stat_out[number, rows, :] = jnp.where(lane < 64, first, second)

    def get_stats(number, rows):
        total = (stat_out[number, rows, :] + stat_in[number, rows, :]) * (1.0 / WIDTH)
        return total[:, 0:1], total[:, 64:65]

    def groups(c, body, unroll=2):
        def one(i, _):
            body(pl.multiple_of(ROWS * c + GROUP * i, GROUP))
            return 0

        lax.fori_loop(0, ROWS // GROUP, one, 0, unroll=unroll)

    def conv_stats(c):
        def body(first):
            rows = pl.ds(first, GROUP)
            strips = [cb[j, rows, :] for j in range(6)]
            total, square = strips[0], strips[0] * strips[0]
            for strip in strips[1:]:
                total, square = total + strip, square + strip * strip
            put_stats(0, rows, jnp.sum(total, -1, keepdims=True), jnp.sum(square, -1, keepdims=True))

        groups(c, body)
        stat_copy(0, c).start()

    for c in (1, 0, 2):
        if c == 0:
            halo_end(h_halo, hb)
        convolve(hb, c, lambda k: k)
        conv_stats(c)

    def activate(c):
        stat_copy(0, c).wait_recv()

        def body(first):
            rows = pl.ds(first, GROUP)
            mean, square = get_stats(0, rows)
            scale = lax.rsqrt(square - mean * mean + epsilon)
            rstd2[rows, :] = jnp.broadcast_to(scale, (GROUP, 128))
            total = cross = None
            for j in range(6):
                columns = slice(128 * j, 128 * j + 128)
                zhat = (cb[j, rows, :] - mean) * scale
                s = sigmoid(zhat)
                cb[j, rows, :] = zhat
                swish = zhat * s
                sw[rows, columns] = swish.astype(BF16)
                slope = ds[rows, columns] * (s + swish * (1.0 - s))
                ds[rows, columns] = slope
                total = slope if total is None else total + slope
                cross = slope * zhat if cross is None else cross + slope * zhat
            put_stats(1, rows, jnp.sum(total, -1, keepdims=True), jnp.sum(cross, -1, keepdims=True))

        groups(c, body)
        stat_copy(1, c).start()

    for c in (1, 0, 2):
        activate(c)

    def part_copy(number, c):
        at = 3 * number + c
        return remote(
            part_out.at[number, chunk(c)], part_in.at[number, chunk(c)], part_send.at[at], part_recv.at[at], partner
        )

    for c in range(CHUNKS):
        for n in range(3):
            part_out[0, chunk(c), 256 * n : 256 * n + 256] = jnp.dot(
                sw[chunk(c), :], wo[other, :, 256 * n : 256 * n + 256], preferred_element_type=F32
            ).astype(BF16)
        part_copy(0, c).start()
    for c in range(CHUNKS):
        for n in range(3):
            po[chunk(c), 256 * n : 256 * n + 256] = jnp.dot(
                sw[chunk(c), :], wo[me, :, 256 * n : 256 * n + 256], preferred_element_type=F32
            )

    finals = (value_grad, gate_grad, out_grad)
    scatters = [
        [Scatter(torus, g, j, grads, landed, sums, finals, send, recv) for j in range(6)] for g in range(GRADS)
    ]

    def weight_grad(g, rows_of, right, n):
        for m in range(4):
            term = dot(rows_of(m), right[:, 256 * n : 256 * n + 256], ((0,), (0,)))
            for half in range(2):
                grads[g, 2 * n + half, m // 2, 2 * (m % 2) : 2 * (m % 2) + 2] = (
                    term[:, 128 * half : 128 * half + 128].reshape(2, 4, 2, 24, 128).astype(BF16)
                )
        for half in range(2):
            scatters[g][2 * n + half].begin(0)

    for n in range(3):
        weight_grad(2, lambda m: uf[m // 2, :, 384 * (m % 2) : 384 * (m % 2) + 384], sw, n)

    def conv_slope(c):
        stat_copy(1, c).wait_recv()

        def body(first):
            rows = pl.ds(first, GROUP)
            mean, cross = get_stats(1, rows)
            scale = rstd2[rows, :]
            for j in range(6):
                slope = scale * (ds[rows, 128 * j : 128 * j + 128] - mean - cb[j, rows, :] * cross)
                db[j, pl.ds(pl.multiple_of(first + EDGE, GROUP), GROUP), :] = slope.astype(BF16).astype(F32)

        groups(c, body)

    conv_slope(0)
    conv_slope(2)
    d_halo = halo(db, 2)
    for copy in d_halo:
        copy.start()
    conv_slope(1)

    def tap_terms(j, _):
        totals = [jnp.zeros((8, 128), F32) for _ in range(TAPS)]
        for c in range(CHUNKS):
            for block in range(SPREAD // 8):
                slopes = [spread(db, j, c, 8 * block + i) for i in range(8)]
                for m in range(8 + TAPS - 1):
                    shifted = spread(hb, j, c, 8 * block + m - REACH)
                    for i in range(max(0, m - TAPS + 1), min(8, m + 1)):
                        totals[m - i] = totals[m - i] + shifted * slopes[i]
        for k in range(TAPS):
            tap_acc[j, k, :] = jnp.sum(totals[k], 0)
        tap_acc[j, TAPS, :] = jnp.zeros((128,), F32)
        return 0

    lax.fori_loop(0, 6, tap_terms, 0)
    tap_sums = [TapSum(torus, color, slots, tap_send, tap_recv) for color in range(3)]
    for color in range(3):
        tap_sums[color].begin(0, tap_acc[2 * color : 2 * color + 2])

    def relay(g, phase):
        for one in scatters[g]:
            one.relay(phase)

    def finish(g, phase):
        for one in scatters[g]:
            one.finish(phase)
            if phase < 2:
                one.begin(phase + 1)

    def tap_step(phase):
        for color in range(3):
            total = tap_sums[color].finish(phase)
            if phase < 2:
                tap_sums[color].begin(phase + 1, total)
            else:
                for half in range(2):
                    j = 2 * color + half
                    taps_grad[:, 128 * j : 128 * j + 128] = total[half]

    relay(2, 0)

    def gate_slopes(c):
        def body(first):
            rows = pl.ds(first, GROUP)
            valid = valid_rows(first, GROUP)
            for j in range(6):
                columns = slice(128 * j, 128 * j + 128)
                sigma = sg[rows, columns]
                slope = cb[j, rows, :] * valid * sigma
                dv[rows, columns] = slope.astype(BF16)
                dg[rows, columns] = (slope * vb[rows, columns] * (1.0 - sigma)).astype(BF16)

        groups(c, body)

    for c in (1, 0, 2):
        if c == 0:
            halo_end(d_halo, db)
        convolve(db, c, lambda k: TAPS - 1 - k)
        gate_slopes(c)
        if c == 1:
            finish(2, 0)
            tap_step(0)
        elif c == 0:
            relay(2, 1)
            tap_step(1)
        else:
            finish(2, 1)
            tap_step(2)

    for n in range(3):
        weight_grad(0, lambda m: nb[:, 384 * m : 384 * m + 384], dv, n)
    relay(2, 2)
    for n in range(3):
        weight_grad(1, lambda m: nb[:, 384 * m : 384 * m + 384], dg, n)
    finish(2, 2)

    def features(c, n, half):
        rows = pl.ds(pl.multiple_of(half * HALF + 256 * n, 256), 256)
        return dot(dv[chunk(c), :], wv[rows, :], ((1,), (1,))) + dot(dg[chunk(c), :], wg[rows, :], ((1,), (1,)))

    for c in range(CHUNKS):
        for n in range(3):
            part_out[1, chunk(c), 256 * n : 256 * n + 256] = features(c, n, other).astype(BF16)
        part_copy(1, c).start()
    relay(0, 0)
    for c in range(CHUNKS):
        for n in range(3):
            vb[chunk(c), 256 * n : 256 * n + 256] = features(c, n, me)
    relay(1, 0)

    def output_rows(c):
        part_copy(0, c).wait_recv()

        def body(first):
            rows = pl.ds(first, GROUP)
            total = xf[me, rows, :].astype(F32) + (po[rows, :] + part_in[0, rows, :].astype(F32))
            xf[me, rows, :] = total.astype(BF16)

        groups(c, body)
        store = pltpu.make_async_copy(xf.at[me, chunk(c)], out.at[chunk(c)], store_sem.at[c])
        store.start()
        return store

    def feature_stats(c):
        part_copy(1, c).wait_recv()

        def body(first):
            rows = pl.ds(first, GROUP)
            slope = vb[rows, :] + part_in[1, rows, :].astype(F32)
            vb[rows, :] = slope
            unit = nb[rows, pl.ds(pl.multiple_of(me * HALF, HALF), HALF)].astype(F32)
            put_stats(2, rows, jnp.sum(slope, -1, keepdims=True), jnp.sum(slope * unit, -1, keepdims=True))

        groups(c, body)
        stat_copy(2, c).start()

    def input_rows(c):
        stat_copy(2, c).wait_recv()

        def body(first):
            rows = pl.ds(first, GROUP)
            mean, cross = get_stats(2, rows)
            scale = rstd1[rows, 0:1]
            unit = nb[rows, pl.ds(pl.multiple_of(me * HALF, HALF), HALF)].astype(F32)
            total = uf[me, rows, :].astype(F32) + scale * (vb[rows, :] - mean - unit * cross)
            uf[me, rows, :] = total.astype(BF16)

        groups(c, body)
        store = pltpu.make_async_copy(uf.at[me, chunk(c)], grad_in.at[chunk(c)], store_sem.at[3 + c])
        store.start()
        return store

    for c in range(CHUNKS):
        feature_stats(c)
    stores = [output_rows(c) for c in range(CHUNKS)]
    finish(0, 0)
    stores += [input_rows(c) for c in range(CHUNKS)]
    finish(1, 0)
    for phase in (1, 2):
        for g in (0, 1):
            relay(g, phase)
        for g in (0, 1):
            finish(g, phase)

    for group in scatters:
        for one in group:
            one.drain()
    for one in tap_sums:
        one.drain()
    for store in stores:
        store.wait()
    for copy in [x_share(c) for c in range(CHUNKS)] + [u_share]:
        copy.wait_send()
    for copy in h_halo + d_halo:
        copy.wait_send()
    for number in range(3):
        for c in range(CHUNKS):
            stat_copy(number, c).wait_send()
    for number in range(2):
        for c in range(CHUNKS):
            part_copy(number, c).wait_send()


def scratch_shapes():
    vmem, dma = pltpu.VMEM, pltpu.SemaphoreType.DMA
    shapes = [vmem((GRADS, 2, 3) + dims + (24, 128), BF16) for order in ORDERS for dims in LEFT[order]]
    shapes += [vmem((GRADS, 2) + dims + (24, 128), BF16) for order in ORDERS for dims in LEFT[order][:2]]
    copies = GRADS * 6 * 9
    shapes += [vmem((3, 3, 4, 2, 32, 128), F32), dma((copies,)), dma((copies,)), dma((27,)), dma((27,))]
    square, padded = (FRAMES, HALF), (6, FRAMES + 2 * EDGE, 128)
    shapes += [
        vmem((GRADS, 6, 2, 4, 4, 2, 24, 128), BF16),
        vmem((2,) + square, BF16),
        vmem((2,) + square, BF16),
        vmem((WIDTH, HALF), BF16),
        vmem((WIDTH, HALF), BF16),
        vmem((2,) + square, BF16),
        vmem((FRAMES, WIDTH), BF16),
        vmem((FRAMES, 128), F32),
        vmem(square, F32),
        vmem(square, F32),
        vmem(padded, F32),
        vmem(padded, F32),
        vmem((6, FRAMES, 128), F32),
        vmem(square, BF16),
        vmem(square, F32),
        vmem((FRAMES, 128), F32),
        vmem((3, FRAMES, 128), F32),
        vmem((3, FRAMES, 128), F32),
        vmem(square, BF16),
        vmem(square, BF16),
        vmem(square, F32),
        vmem((2,) + square, BF16),
        vmem((2,) + square, BF16),
        vmem((6, TAPS, 8, 128), F32),
        vmem((6, TAPS + 1, 128), F32),
        dma((8,)), dma((3,)), dma((3,)), dma(()), dma(()), dma((4,)), dma((4,)),
        dma((9,)), dma((9,)), dma((6,)), dma((6,)), dma((6,)),
    ]
    return shapes


def shards(inputs, lengths, cotangent, w_value, w_gate, kernel_taps, w_out):
    here, vmem = pl.BlockSpec(memory_space=pl.ANY), pl.BlockSpec(memory_space=pltpu.VMEM)
    smem = pl.BlockSpec(memory_space=pltpu.SMEM)
    rows = jax.ShapeDtypeStruct((FRAMES, HALF), BF16)
    block = jax.ShapeDtypeStruct((24, HALF), F32)
    output, input_gradient, value_grad, gate_grad, kernel_grad, out_grad = pl.pallas_call(
        kernel,
        out_shape=(rows, rows, block, block, jax.ShapeDtypeStruct((TAPS + 1, HALF), F32), block),
        in_specs=[smem, here, here, here, here, vmem, here],
        out_specs=(here, here, vmem, vmem, vmem, vmem),
        scratch_shapes=scratch_shapes(),
        compiler_params=pltpu.CompilerParams(
            collective_id=0, has_side_effects=True, vmem_limit_bytes=67043328
        ),
    )(lengths, inputs[0], cotangent[0], w_value, w_gate, kernel_taps, w_out)
    return (output[None], input_gradient[None], value_grad, gate_grad, kernel_grad[:TAPS], out_grad.T)


def solution(mesh):
    return jax.shard_map(
        shards,
        mesh=mesh,
        in_specs=(
            P("dp", "seq", "tensor"),
            P("dp"),
            P("dp", "seq", "tensor"),
            P(None, "tensor"),
            P(None, "tensor"),
            P(None, "tensor"),
            P("tensor", None),
        ),
        out_specs=(
            P("dp", "seq", "tensor"),
            P("dp", "seq", "tensor"),
            P(("seq", "dp"), "tensor"),
            P(("seq", "dp"), "tensor"),
            P(None, "tensor"),
            P("tensor", ("seq", "dp")),
        ),
        check_vma=False,
    )
```

profile of v0, /device:TPU:0, one launch (start us, length us, event | category | flops | bytes accessed | tf_op | source)
XLA Modules:
  0.0 123.1 jit_solution(1829696500307401103)
XLA Ops:
  1.3 115.8 %shard_map.118 = (bf16[768,768]{1,0:T(8,128)(2,1)}, bf16[768,768]{1,0:T(8,128)(2,1)}, f32[24,768]{1,0:T(8,128)}, f32[24,768]{1,0:T(8,128)}, f32[32,768]{1,0:T(8,128)}, /*index=5*/f32[24,768]{1,0:T(8,128)}) custom-call(s32[1]{0:T(128)S(6)} %copy.19.lengths, bf16[768,768]{1,0:T(8,128)(2,1)} %bitcast.6, bf16[768,768]{1,0:T(8,128)(2,1)} %bitcast.7, ...), custom_call_target="tpu_custom_call" | custom-call | tf_op jit(solution)/shard_map/pallas_call | solution.py:670
  117.1 0.0 copy-start
  117.1 2.5 %copy.20 = bf16[1,768,768]{2,1,0:T(8,128)(2,1)} copy(bf16[1,768,768]{2,1,0:T(8,128)(2,1)} %bitcast.9) | data formatting | bytes 2359296
  119.5 0.0 copy-done
  119.5 0.0 copy-start.4
  119.5 0.0 copy-start.3
  119.5 0.0 copy-start.1
  119.5 0.0 copy-start.2
  119.6 1.0 copy.21
  120.6 0.0 copy-done.4
  120.6 0.6 copy.22
  121.2 0.0 copy-done.3
  121.2 0.6 copy.23
  121.8 0.0 copy-done.1
  121.9 0.6 copy.24
  122.5 0.0 copy-done.2
  122.5 0.6 copy.25
Async XLA Ops:
  117.1 2.5 %copy-start = (bf16[768,768]{1,0:T(8,128)(2,1)S(1)}, bf16[768,768]{1,0:T(8,128)(2,1)}, u32[]{:S(2)}) copy-start(bf16[768,768]{1,0:T(8,128)(2,1)} %get-tuple-element.13) | copy-start | bytes 3538948
  119.5 1.0 copy-start.4
  119.5 1.7 %copy-start.3 = (f32[24,768]{1,0:T(8,128)S(1)}, f32[24,768]{1,0:T(8,128)}, u32[]{:S(2)}) copy-start(f32[24,768]{1,0:T(8,128)} %get-tuple-element.27) | copy-start | bytes 221188
  119.5 2.3 %copy-start.1 = (f32[32,768]{1,0:T(8,128)S(1)}, f32[32,768]{1,0:T(8,128)}, u32[]{:S(2)}) copy-start(f32[32,768]{1,0:T(8,128)} %get-tuple-element.16) | copy-start | bytes 294916
  119.5 2.9 %copy-start.2 = (f32[24,768]{1,0:T(8,128)S(1)}, f32[24,768]{1,0:T(8,128)}, u32[]{:S(2)}) copy-start(f32[24,768]{1,0:T(8,128)} %get-tuple-element.17) | copy-start | bytes 221188
where the time goes:
time: 123 us
  Pallas kernels  116 us (94%)
  local copies, waits for them, and re-layouts  6.03 us (5%)
  between operations  1.31 us (1%)
    pallas_call x1, Pallas kernels, shards(): pl.pallas_call(kernel, out_shape=(rows, rows, block, block, jax.ShapeDtyp...  116 us
    unnamed x16, local copies, waits for them, and re-layouts  6.03 us

commit v1 on v0

--- a/solution.py
+++ b/solution.py
@@ -15,7 +15,7 @@
 FRAMES, WIDTH, HALF = 768, 1536, 768
 ROWS, CHUNKS = 256, 3
 GROUP = 16
-SPREAD = ROWS // 8
+BLOCK = 32
 TAPS, REACH, EDGE = 31, 15, 16
 LEFT = {
     "xyz": ((4, 4), (4,), ()),
@@ -228,7 +228,7 @@
         pltpu.make_async_copy(w_out.at[:, pl.ds(HALF * h, HALF)], wo.at[h], load_sem.at[6 + h])
         for h in range(2)
     ]
-    for c in range(CHUNKS):
+    for c in (0, 2, 1):
         x_load(c).start()
     wv_load.start()
     wg_load.start()
@@ -236,7 +236,7 @@
     for load in wo_loads:
         load.start()
     greet(torus)
-    for c in range(CHUNKS):
+    for c in (0, 2, 1):
         x_share(c).start()
     u_share.start()
 
@@ -245,12 +245,19 @@
         for k in range(TAPS):
             tap_wide[j, k] = jnp.broadcast_to(tap_rows[k : k + 1, 128 * j : 128 * j + 128], (8, 128))
 
-    for c in range(CHUNKS):
+    def groups(c, body, unroll=4):
+        def one(i, _):
+            body(pl.multiple_of(ROWS * c + GROUP * i, GROUP))
+            return 0
+
+        lax.fori_loop(0, ROWS // GROUP, one, 0, unroll=unroll)
+
+    def normalize(c):
         x_load(c).wait()
         x_share(c).wait_recv()
 
-        def normalize(i, _, c=c):
-            rows = pl.ds(pl.multiple_of(ROWS * c + GROUP * i, GROUP), GROUP)
+        def body(first):
+            rows = pl.ds(first, GROUP)
             a, b = xf[0, rows, :].astype(F32), xf[1, rows, :].astype(F32)
             mean = (jnp.sum(a, -1, keepdims=True) + jnp.sum(b, -1, keepdims=True)) / WIDTH
             a, b = a - mean, b - mean
@@ -259,12 +266,9 @@
             nb[rows, 0:HALF] = (a * scale).astype(BF16)
             nb[rows, HALF:WIDTH] = (b * scale).astype(BF16)
             rstd1[rows, :] = jnp.broadcast_to(scale, (GROUP, 128))
-            return 0
-
-        lax.fori_loop(0, ROWS // GROUP, normalize, 0, unroll=2)
-
-    wv_load.wait()
-    wg_load.wait()
+
+        groups(c, body)
+
     length = lengths[0]
 
     def valid_rows(first, count):
@@ -301,13 +305,68 @@
             copy.wait_recv()
             buf[:, rows, :] = buf[:, rows, :] * keep
 
+    normalize(0)
+    wv_load.wait()
+    wg_load.wait()
     gate(0)
+    normalize(2)
     gate(2)
     h_halo = halo(hb, 0)
     for copy in h_halo:
         copy.start()
+    normalize(1)
     gate(1)
 
+    def near(buf, j, row):
+        return buf[j, pl.ds(row, 8), :]
+
+    def convolve(buf, c, tap_at):
+        def strip(j, _):
+            def block(b, _):
+                first = pl.multiple_of(ROWS * c + BLOCK * b, BLOCK)
+                totals = [None] * (BLOCK // 8)
+                for k in range(TAPS):
+                    tap = tap_wide[j, tap_at(k)]
+                    for i in range(BLOCK // 8):
+                        term = near(buf, j, first + (EDGE - REACH + k + 8 * i)) * tap
+                        totals[i] = term if k == 0 else totals[i] + term
+                for i in range(BLOCK // 8):
+                    cb[j, pl.ds(pl.multiple_of(first + 8 * i, 8), 8), :] = totals[i]
+                return 0
+
+            return lax.fori_loop(0, ROWS // BLOCK, block, 0)
+
+        lax.fori_loop(0, 6, strip, 0)
+
+    lane = lax.broadcasted_iota(jnp.int32, (GROUP, 128), 1)
+
+    def stat_copy(number, c):
+        at = 3 * number + c
+        return remote(
+            stat_out.at[number, chunk(c)], stat_in.at[number, chunk(c)], stat_send.at[at], stat_recv.at[at], partner
+        )
+
+    def put_stats(number, rows, first, second):
+        stat_out[number, rows, :] = jnp.where(lane < 64, first, second)
+
+    def get_stats(number, rows):
+        total = (stat_out[number, rows, :] + stat_in[number, rows, :]) * (1.0 / WIDTH)
+        return total[:, 0:1], total[:, 64:65]
+
+    def conv_stats(c):
+        def body(first):
+            rows = pl.ds(first, GROUP)
+            strips = [cb[j, rows, :] for j in range(6)]
+            total, square = strips[0], strips[0] * strips[0]
+            for strip in strips[1:]:
+                total, square = total + strip, square + strip * strip
+            put_stats(0, rows, jnp.sum(total, -1, keepdims=True), jnp.sum(square, -1, keepdims=True))
+
+        groups(c, body)
+        stat_copy(0, c).start()
+
+    convolve(hb, 1, lambda k: k)
+    conv_stats(1)
     u_load.wait()
     u_share.wait_recv()
     for load in wo_loads:
@@ -317,62 +376,8 @@
             ds[chunk(c), 256 * n : 256 * n + 256] = dot(
                 uf[0, chunk(c), :], wo[0, 256 * n : 256 * n + 256, :], ((1,), (1,))
             ) + dot(uf[1, chunk(c), :], wo[1, 256 * n : 256 * n + 256, :], ((1,), (1,)))
-
-    def spread(buf, j, c, r):
-        return buf[j, pl.ds(EDGE + ROWS * c + r, 8, stride=SPREAD), :]
-
-    def convolve(buf, c, tap_at):
-        def strip(j, _):
-            for block in range(SPREAD // 8):
-                totals = [None] * 8
-                for m in range(8 + TAPS - 1):
-                    shifted = spread(buf, j, c, 8 * block + m - REACH)
-                    for i in range(max(0, m - TAPS + 1), min(8, m + 1)):
-                        term = shifted * tap_wide[j, tap_at(m - i)]
-                        totals[i] = term if totals[i] is None else totals[i] + term
-                for i in range(8):
-                    cb[j, pl.ds(ROWS * c + 8 * block + i, 8, stride=SPREAD), :] = totals[i]
-            return 0
-
-        lax.fori_loop(0, 6, strip, 0)
-
-    lane = lax.broadcasted_iota(jnp.int32, (GROUP, 128), 1)
-
-    def stat_copy(number, c):
-        at = 3 * number + c
-        return remote(
-            stat_out.at[number, chunk(c)], stat_in.at[number, chunk(c)], stat_send.at[at], stat_recv.at[at], partner
-        )
-
-    def put_stats(number, rows, first, second):
-        stat_out[number, rows, :] = jnp.where(lane < 64, first, second)
-
-    def get_stats(number, rows):
-        total = (stat_out[number, rows, :] + stat_in[number, rows, :]) * (1.0 / WIDTH)
-        return total[:, 0:1], total[:, 64:65]
-
-    def groups(c, body, unroll=2):
-        def one(i, _):
-            body(pl.multiple_of(ROWS * c + GROUP * i, GROUP))
-            return 0
-
-        lax.fori_loop(0, ROWS // GROUP, one, 0, unroll=unroll)
-
-    def conv_stats(c):
-        def body(first):
-            rows = pl.ds(first, GROUP)
-            strips = [cb[j, rows, :] for j in range(6)]
-            total, square = strips[0], strips[0] * strips[0]
-            for strip in strips[1:]:
-                total, square = total + strip, square + strip * strip
-            put_stats(0, rows, jnp.sum(total, -1, keepdims=True), jnp.sum(square, -1, keepdims=True))
-
-        groups(c, body)
-        stat_copy(0, c).start()
-
-    for c in (1, 0, 2):
-        if c == 0:
-            halo_end(h_halo, hb)
+    halo_end(h_halo, hb)
+    for c in (0, 2):
         convolve(hb, c, lambda k: k)
         conv_stats(c)
 
@@ -410,18 +415,6 @@
             part_out.at[number, chunk(c)], part_in.at[number, chunk(c)], part_send.at[at], part_recv.at[at], partner
         )
 
-    for c in range(CHUNKS):
-        for n in range(3):
-            part_out[0, chunk(c), 256 * n : 256 * n + 256] = jnp.dot(
-                sw[chunk(c), :], wo[other, :, 256 * n : 256 * n + 256], preferred_element_type=F32
-            ).astype(BF16)
-        part_copy(0, c).start()
-    for c in range(CHUNKS):
-        for n in range(3):
-            po[chunk(c), 256 * n : 256 * n + 256] = jnp.dot(
-                sw[chunk(c), :], wo[me, :, 256 * n : 256 * n + 256], preferred_element_type=F32
-            )
-
     finals = (value_grad, gate_grad, out_grad)
     scatters = [
         [Scatter(torus, g, j, grads, landed, sums, finals, send, recv) for j in range(6)] for g in range(GRADS)
@@ -460,23 +453,29 @@
         copy.start()
     conv_slope(1)
 
-    def tap_terms(j, _):
-        totals = [jnp.zeros((8, 128), F32) for _ in range(TAPS)]
-        for c in range(CHUNKS):
-            for block in range(SPREAD // 8):
-                slopes = [spread(db, j, c, 8 * block + i) for i in range(8)]
-                for m in range(8 + TAPS - 1):
-                    shifted = spread(hb, j, c, 8 * block + m - REACH)
-                    for i in range(max(0, m - TAPS + 1), min(8, m + 1)):
-                        totals[m - i] = totals[m - i] + shifted * slopes[i]
+    def tap_terms(j):
+        def block(b, totals):
+            first = pl.multiple_of(BLOCK * b, BLOCK)
+            slopes = [near(db, j, pl.multiple_of(first + (EDGE + 8 * i), 8)) for i in range(BLOCK // 8)]
+            totals = list(totals)
+            for m in range(BLOCK - 8 + TAPS):
+                shifted = near(hb, j, first + (EDGE - REACH + m))
+                for i in range(BLOCK // 8):
+                    if 0 <= m - 8 * i < TAPS:
+                        totals[m - 8 * i] = totals[m - 8 * i] + shifted * slopes[i]
+            return tuple(totals)
+
+        zeros = tuple(jnp.zeros((8, 128), F32) for _ in range(TAPS))
+        totals = lax.fori_loop(0, FRAMES // BLOCK, block, zeros)
         for k in range(TAPS):
             tap_acc[j, k, :] = jnp.sum(totals[k], 0)
         tap_acc[j, TAPS, :] = jnp.zeros((128,), F32)
-        return 0
-
-    lax.fori_loop(0, 6, tap_terms, 0)
+
     tap_sums = [TapSum(torus, color, slots, tap_send, tap_recv) for color in range(3)]
-    for color in range(3):
+
+    def tap_color(color):
+        for j in (2 * color, 2 * color + 1):
+            tap_terms(j)
         tap_sums[color].begin(0, tap_acc[2 * color : 2 * color + 2])
 
     def relay(g, phase):
@@ -499,7 +498,6 @@
                     j = 2 * color + half
                     taps_grad[:, 128 * j : 128 * j + 128] = total[half]
 
-    relay(2, 0)
 
     def gate_slopes(c):
         def body(first):
@@ -514,41 +512,50 @@
 
         groups(c, body)
 
-    for c in (1, 0, 2):
-        if c == 0:
-            halo_end(d_halo, db)
+    convolve(db, 1, lambda k: TAPS - 1 - k)
+    gate_slopes(1)
+    relay(2, 0)
+    halo_end(d_halo, db)
+    for c in (0, 2):
         convolve(db, c, lambda k: TAPS - 1 - k)
         gate_slopes(c)
-        if c == 1:
-            finish(2, 0)
-            tap_step(0)
-        elif c == 0:
-            relay(2, 1)
-            tap_step(1)
-        else:
-            finish(2, 1)
-            tap_step(2)
+    finish(2, 0)
 
     for n in range(3):
         weight_grad(0, lambda m: nb[:, 384 * m : 384 * m + 384], dv, n)
-    relay(2, 2)
+    relay(2, 1)
     for n in range(3):
         weight_grad(1, lambda m: nb[:, 384 * m : 384 * m + 384], dg, n)
-    finish(2, 2)
 
     def features(c, n, half):
         rows = pl.ds(pl.multiple_of(half * HALF + 256 * n, 256), 256)
         return dot(dv[chunk(c), :], wv[rows, :], ((1,), (1,))) + dot(dg[chunk(c), :], wg[rows, :], ((1,), (1,)))
 
-    for c in range(CHUNKS):
-        for n in range(3):
-            part_out[1, chunk(c), 256 * n : 256 * n + 256] = features(c, n, other).astype(BF16)
-        part_copy(1, c).start()
-    relay(0, 0)
-    for c in range(CHUNKS):
-        for n in range(3):
-            vb[chunk(c), 256 * n : 256 * n + 256] = features(c, n, me)
-    relay(1, 0)
+    def features_over():
+        for c in range(CHUNKS):
+            for n in range(3):
+                part_out[1, chunk(c), 256 * n : 256 * n + 256] = features(c, n, other).astype(BF16)
+            part_copy(1, c).start()
+
+    def features_here():
+        for c in range(CHUNKS):
+            for n in range(3):
+                vb[chunk(c), 256 * n : 256 * n + 256] = features(c, n, me)
+
+    def output_over():
+        for c in range(CHUNKS):
+            for n in range(3):
+                part_out[0, chunk(c), 256 * n : 256 * n + 256] = jnp.dot(
+                    sw[chunk(c), :], wo[other, :, 256 * n : 256 * n + 256], preferred_element_type=F32
+                ).astype(BF16)
+            part_copy(0, c).start()
+
+    def output_here():
+        for c in range(CHUNKS):
+            for n in range(3):
+                po[chunk(c), 256 * n : 256 * n + 256] = jnp.dot(
+                    sw[chunk(c), :], wo[me, :, 256 * n : 256 * n + 256], preferred_element_type=F32
+                )
 
     def output_rows(c):
         part_copy(0, c).wait_recv()
@@ -592,17 +599,35 @@
         store.start()
         return store
 
+    tap_color(0)
+    relay(0, 0)
+    tap_color(1)
+    finish(2, 1)
+    tap_color(2)
+    relay(1, 0)
+    relay(2, 2)
+    features_over()
+    finish(0, 0)
+    tap_step(0)
+    features_here()
+    finish(1, 0)
+    finish(2, 2)
+    output_over()
+    relay(0, 1)
+    tap_step(1)
+    output_here()
+    relay(1, 1)
     for c in range(CHUNKS):
         feature_stats(c)
+    finish(0, 1)
+    tap_step(2)
     stores = [output_rows(c) for c in range(CHUNKS)]
-    finish(0, 0)
+    finish(1, 1)
     stores += [input_rows(c) for c in range(CHUNKS)]
-    finish(1, 0)
-    for phase in (1, 2):
-        for g in (0, 1):
-            relay(g, phase)
-        for g in (0, 1):
-            finish(g, phase)
+    relay(0, 2)
+    relay(1, 2)
+    finish(0, 2)
+    finish(1, 2)
 
     for group in scatters:
         for one in group:
@@ -621,6 +646,33 @@
     for number in range(2):
         for c in range(CHUNKS):
             part_copy(number, c).wait_send()
+
+
+def place_kernel(out, grad_in, value, gate, taps, outer, out_to, grad_in_to, value_to, gate_to, taps_to, outer_to, buf, load, store):
+    def copies(source, target, n):
+        found = []
+        for c in range(CHUNKS):
+            rows = pl.ds(ROWS * c, ROWS)
+            found.append(
+                (
+                    pltpu.make_async_copy(source.at[rows], buf.at[n, rows], load.at[n, c]),
+                    pltpu.make_async_copy(buf.at[n, rows], target.at[rows], store.at[n, c]),
+                )
+            )
+        return found
+
+    pairs = copies(out, out_to, 0) + copies(grad_in, grad_in_to, 1)
+    for first, _ in pairs:
+        first.start()
+    value_to[...] = value[...]
+    gate_to[...] = gate[...]
+    taps_to[...] = taps[0:TAPS, :]
+    outer_to[...] = outer[...]
+    for first, second in pairs:
+        first.wait()
+        second.start()
+    for _, second in pairs:
+        second.wait()
 
 
 def scratch_shapes():
@@ -677,7 +729,18 @@
             collective_id=0, has_side_effects=True, vmem_limit_bytes=67043328
         ),
     )(lengths, inputs[0], cotangent[0], w_value, w_gate, kernel_taps, w_out)
-    return (output[None], input_gradient[None], value_grad, gate_grad, kernel_grad[:TAPS], out_grad.T)
+    output, input_gradient, value_grad, gate_grad, kernel_grad, out_grad = pl.pallas_call(
+        place_kernel,
+        out_shape=(rows, rows, block, block, jax.ShapeDtypeStruct((TAPS, HALF), F32), block),
+        in_specs=[here, here, vmem, vmem, vmem, vmem],
+        out_specs=(here, here, vmem, vmem, vmem, vmem),
+        scratch_shapes=[
+            pltpu.VMEM((2, FRAMES, HALF), BF16),
+            pltpu.SemaphoreType.DMA((2, CHUNKS)),
+            pltpu.SemaphoreType.DMA((2, CHUNKS)),
+        ],
+    )(output, input_gradient, value_grad, gate_grad, kernel_grad, out_grad)
+    return (output[None], input_gradient[None], value_grad, gate_grad, kernel_grad, out_grad.T)
 
 
 def solution(mesh):

time: 123 us -> 96.1 us (0.78)
  Pallas kernels: 116 us -> 94.4 us
  local copies, waits for them, and re-layouts: 6.03 us -> 0 us
    pallas_call x1, Pallas kernels: 116 us -> 90.2 us  [shards(): pl.pallas_call(kernel, out_shape=(rows, rows, block, block, jax.ShapeDtyp...]
    unnamed x16 -> x0, local copies, waits for them, and re-layouts: 6.03 us -> none
    pallas_call x0 -> x1, Pallas kernels: none -> 4.21 us  [shards(): pl.pallas_call(place_kernel, out_shape=(rows, rows, block, block, jax.Sha...]
where the time goes in v1:
time: 96.1 us; the launch traced here: 95.9 us
  Pallas kernels  94.4 us (98%)
  between operations  1.45 us (2%)
    pallas_call x1, Pallas kernels, shards(): pl.pallas_call(kernel, out_shape=(rows, rows, block, block, jax.ShapeDtyp...  90.2 us
    pallas_call x1, Pallas kernels, shards(): pl.pallas_call(place_kernel, out_shape=(rows, rows, block, block, jax.Sha...  4.21 us

profile of v1, /device:TPU:0, one launch (start us, length us, event | category | flops | bytes accessed | tf_op | source)
XLA Modules:
  0.0 95.9 jit_solution(17693973796275392902)
XLA Ops:
  1.3 90.2 %shard_map.118 = (bf16[768,768]{1,0:T(8,128)(2,1)}, bf16[768,768]{1,0:T(8,128)(2,1)}, f32[24,768]{1,0:T(8,128)}, f32[24,768]{1,0:T(8,128)}, f32[32,768]{1,0:T(8,128)}, /*index=5*/f32[24,768]{1,0:T(8,128)}) custom-call(s32[1]{0:T(128)S(6)} %copy.13.lengths, bf16[768,768]{1,0:T(8,128)(2,1)} %bitcast.5, bf16[768,768]{1,0:T(8,128)(2,1)} %bitcast.6, ...), custom_call_target="tpu_custom_call" | custom-call | tf_op jit(solution)/shard_map/pallas_call | solution.py:722
  91.5 4.2 %shard_map.119 = (bf16[768,768]{1,0:T(8,128)(2,1)}, bf16[768,768]{1,0:T(8,128)(2,1)}, f32[24,768]{1,0:T(8,128)}, f32[24,768]{1,0:T(8,128)}, f32[31,768]{1,0:T(8,128)}, /*index=5*/f32[24,768]{1,0:T(8,128)}) custom-call(bf16[768,768]{1,0:T(8,128)(2,1)} %get-tuple-element.18.out, bf16[768,768]{1,0:T(8,128)(2,1)} %get-tuple-element.19.grad_in, ...), custom_call_target="tpu_custom_call" | custom-call | tf_op jit(solution)/shard_map/pallas_call | solution.py:732

commit v2 on v1

v2 whole, which is shorter than its diff:
```python
import jax
import jax.numpy as jnp
from jax import lax
from jax.experimental import pallas as pl
from jax.experimental.pallas import tpu as pltpu
from jax.sharding import PartitionSpec as P

epsilon = 1e-05
MESH = pl.DeviceIdType.MESH
BF16, F32 = jnp.bfloat16, jnp.float32
ORDERS = ("xyz", "yzx", "zxy")
GRADS = 3
FRAMES, WIDTH, HALF = 768, 1536, 768
ROWS, CHUNKS = 256, 3
GROUP = 16
BLOCK = 32
TAPS, REACH, EDGE = 31, 15, 16
LEFT = {
    "xyz": ((4, 4), (4,), ()),
    "yzx": ((2, 4, 2), (2, 2), ()),
    "zxy": ((2, 4, 2), (4,), ()),
}


class Torus:
    def __init__(self):
        seq, low = lax.axis_index("seq"), lax.axis_index("dp")
        self.at = {
            "x": lax.div(seq, 16) * 2 + low,
            "y": lax.rem(seq, 4),
            "z": lax.rem(lax.div(seq, 4), 4),
        }

    def moved(self, axis, by):
        return lax.rem(self.at[axis] + (by + 4), 4)

    def beside(self, by):
        return {"seq": lax.rem(lax.axis_index("seq") + (by + 32), 32)}

    def peer(self, axis, by):
        at = dict(self.at)
        at[axis] = self.moved(axis, by)
        return {
            "seq": (lax.div(at["x"], 2) * 4 + at["z"]) * 4 + at["y"],
            "dp": lax.rem(at["x"], 2),
        }


def part_of(order, phase, coord):
    every = slice(None)
    high, low = lax.div(coord, 2), lax.rem(coord, 2)
    if phase == 0:
        return {
            "x": (high, every, every, low),
            "y": (every, every, coord, every),
            "z": (every, coord, every, every),
        }[order[0]]
    if phase == 1:
        return {"xyz": (every, coord), "yzx": (every, coord, every), "zxy": (high, every, low)}[order]
    return {"xyz": (coord,), "yzx": (high, low), "zxy": (coord,)}[order]


def wait_bytes(torus, ref, sem, sent=False):
    copy = pltpu.make_async_remote_copy(
        src_ref=ref, dst_ref=ref, send_sem=sem, recv_sem=sem, device_id=torus.peer("x", 1), device_id_type=MESH
    )
    if sent:
        copy.wait_send()
    else:
        copy.wait_recv()


class Scatter:
    def __init__(self, torus, grad, color, source, landed, sums, out, send, recv):
        self.torus, self.grad, self.color = torus, grad, color
        self.source, self.landed, self.sums, self.out = source, landed[color], sums[color], out
        self.sent, self.recv = send, recv
        self.order = ORDERS[color]

    def held(self, phase, half, by):
        part = part_of(self.order, phase, self.torus.moved(self.order[phase], by))
        if phase == 0:
            return self.source.at[(self.grad, 2 * self.color + half) + part]
        return self.sums[phase - 1].at[(self.grad, half) + part]

    def arrived(self, phase, late=1):
        return self.recv.at[(self.grad * 3 + self.color) * 4 + (late if phase == 0 else phase + 1)]

    def send(self, phase, half, which, ref, by):
        return pltpu.make_async_remote_copy(
            src_ref=ref,
            dst_ref=self.landed[phase].at[self.grad, half, which],
            send_sem=self.sent.at[self.color * 3 + phase],
            recv_sem=self.arrived(phase, 0 if which == 0 else 1),
            device_id=self.torus.peer(self.order[phase], by),
            device_id_type=MESH,
        )

    def begin(self, phase):
        for half, way in ((0, 1), (1, -1)):
            if phase == 0:
                self.send(0, half, 0, self.held(0, half, 2), way).start()
                self.send(0, half, 1, self.held(0, half, -way), -way).start()
            else:
                for which, by in enumerate((2, -way, way)):
                    self.send(phase, half, which, self.held(phase, half, by), by).start()

    def relay(self):
        wait_bytes(self.torus, self.landed[0].at[self.grad, :, 0], self.arrived(0, 0))
        for half, way in ((0, 1), (1, -1)):
            slot = self.landed[0].at[self.grad, half, 0]
            slot[...] = (slot[...].astype(F32) + self.held(0, half, way)[...].astype(F32)).astype(BF16)
            self.send(0, half, 2, slot, way).start()

    def finish(self, phase):
        first = 1 if phase == 0 else 0
        wait_bytes(self.torus, self.landed[phase].at[self.grad, :, first:3], self.arrived(phase))
        for half in range(2):
            total = self.held(phase, half, 0)[...].astype(F32)
            for which in range(first, 3):
                total = total + self.landed[phase][self.grad, half, which].astype(F32)
            if phase < 2:
                self.sums[phase][self.grad, half] = total.astype(BF16)
            else:
                strip = 2 * self.color + half
                self.out[self.grad][:, 128 * strip : 128 * strip + 128] = total
        if phase < 2:
            self.begin(phase + 1)


class TapSum:
    def __init__(self, torus, color, slots, send, recv):
        self.torus, self.color, self.slots, self.send, self.recv = torus, color, slots, send, recv
        self.order = ORDERS[color]

    def begin(self, phase, value):
        axis = self.order[phase]
        here = self.slots.at[self.color, phase, self.torus.at[axis]]
        here[...] = value.astype(BF16)
        for by in (1, 3, 2):
            pltpu.make_async_remote_copy(
                src_ref=here,
                dst_ref=here,
                send_sem=self.send,
                recv_sem=self.recv.at[self.color * 3 + phase],
                device_id=self.torus.peer(axis, by),
                device_id_type=MESH,
            ).start()

    def finish(self, phase):
        wait_bytes(self.torus, self.slots.at[self.color, phase, 0:3], self.recv.at[self.color * 3 + phase])
        slots = self.slots
        total = slots[self.color, phase, 0].astype(F32)
        for place in (1, 2, 3):
            total = total + slots[self.color, phase, place].astype(F32)
        return total


def greet(torus):
    barrier = pltpu.get_barrier_semaphore()
    peers = [torus.peer(axis, by) for axis in "xyz" for by in (1, 2, 3)]
    peers += [torus.beside(1), torus.beside(-1), {"tensor": 1 - lax.axis_index("tensor")}]
    for peer in peers:
        pl.semaphore_signal(barrier, inc=1, device_id=peer, device_id_type=MESH)
    pl.semaphore_wait(barrier, len(peers))


def sigmoid(values):
    return 0.5 * jnp.tanh(0.5 * values) + 0.5


def dot(a, b, contract):
    return lax.dot_general(a, b, (contract, ((), ())), preferred_element_type=F32)


def kernel(lengths, x, cot, w_value, w_gate, taps_in, w_out, out, grad_in, value_out, gate_out, taps_out, outer_out, *scratch):
    landed = [scratch[3 * c : 3 * c + 3] for c in range(3)]
    sums = [scratch[9 + 2 * c : 11 + 2 * c] for c in range(3)]
    (
        slots, send, recv, tap_send, tap_recv,
        grads, xf, uf, wv, wg, wo, nb, rstd1, vb, sg, hb, db, cb, sw, ds, rstd2, stat_out, stat_in,
        dv, dg, po, part_out, part_in, taps, length, tap_wide, tap_acc, value_grad, gate_grad, out_grad, taps_grad,
        load_sem, x_send, x_recv, u_send, u_recv, halo_send, halo_recv, stat_send, stat_recv, part_send, part_recv, store_sem,
    ) = scratch[15:]
    torus = Torus()
    me = lax.axis_index("tensor")
    other = 1 - me
    partner = {"tensor": other}
    seq = lax.axis_index("seq")

    def remote(src, dst, send_sem, recv_sem, to):
        return pltpu.make_async_remote_copy(
            src_ref=src, dst_ref=dst, send_sem=send_sem, recv_sem=recv_sem, device_id=to, device_id_type=MESH
        )

    def chunk(c):
        return pl.ds(ROWS * c, ROWS)

    def x_load(c):
        return pltpu.make_async_copy(x.at[chunk(c)], xf.at[me, chunk(c)], load_sem.at[c])

    def x_share(c):
        return remote(x.at[chunk(c)], xf.at[me, chunk(c)], x_send, x_recv.at[c], partner)

    tap_load = pltpu.make_async_copy(taps_in, taps, load_sem.at[8])
    length_load = pltpu.make_async_copy(lengths, length, load_sem.at[9])
    u_load = pltpu.make_async_copy(cot, uf.at[me], load_sem.at[3])
    u_share = remote(cot, uf.at[me], u_send, u_recv, partner)
    wv_load = pltpu.make_async_copy(w_value, wv, load_sem.at[4])
    wg_load = pltpu.make_async_copy(w_gate, wg, load_sem.at[5])
    wo_loads = [
        pltpu.make_async_copy(w_out.at[:, pl.ds(HALF * h, HALF)], wo.at[h], load_sem.at[6 + h])
        for h in range(2)
    ]
    for c in (0, 2, 1):
        x_load(c).start()
    tap_load.start()
    length_load.start()
    wv_load.start()
    wg_load.start()
    u_load.start()
    for load in wo_loads:
        load.start()
    greet(torus)
    for c in (0, 2, 1):
        x_share(c).start()
    u_share.start()

    tap_load.wait()
    length_load.wait()
    tap_rows = taps[...].astype(F32)
    for j in range(6):
        for k in range(TAPS):
            tap_wide[j, k] = jnp.broadcast_to(tap_rows[k : k + 1, 128 * j : 128 * j + 128], (8, 128))

    def groups(c, body, unroll=8):
        def one(i, _):
            body(pl.multiple_of(ROWS * c + GROUP * i, GROUP))
            return 0

        lax.fori_loop(0, ROWS // GROUP, one, 0, unroll=unroll)

    def normalize(c):
        x_load(c).wait()
        x_share(c).wait_recv()

        def body(first):
            rows = pl.ds(first, GROUP)
            a, b = xf[0, rows, :].astype(F32), xf[1, rows, :].astype(F32)
            mean = (jnp.sum(a, -1, keepdims=True) + jnp.sum(b, -1, keepdims=True)) / WIDTH
            a, b = a - mean, b - mean
            var = (jnp.sum(a * a, -1, keepdims=True) + jnp.sum(b * b, -1, keepdims=True)) / WIDTH
            scale = lax.rsqrt(var + epsilon)
            nb[rows, 0:HALF] = (a * scale).astype(BF16)
            nb[rows, HALF:WIDTH] = (b * scale).astype(BF16)
            rstd1[rows, :] = jnp.broadcast_to(scale, (GROUP, 128))

        groups(c, body)

    frames_valid = jnp.broadcast_to(length[...], (ROWS, 128))

    def valid_rows(first, count):
        position = lax.broadcasted_iota(jnp.int32, (count, 128), 0) + (seq * FRAMES + first)
        return jnp.where(position < frames_valid[0:count], 1.0, 0.0)

    def gate(c):
        for n in range(3):
            columns = slice(256 * n, 256 * n + 256)
            values = jnp.dot(nb[chunk(c), :], wv[:, columns], preferred_element_type=F32)
            sigma = sigmoid(jnp.dot(nb[chunk(c), :], wg[:, columns], preferred_element_type=F32))
            valid = valid_rows(ROWS * c, ROWS)
            vb[chunk(c), columns] = values
            sg[chunk(c), columns] = sigma
            for half in range(2):
                strip = slice(128 * half, 128 * half + 128)
                hidden = values[:, strip] * sigma[:, strip] * valid
                hb[2 * n + half, pl.ds(EDGE + ROWS * c, ROWS), :] = hidden.astype(BF16).astype(F32)

    def halo(buf, number):
        first, last = pl.ds(EDGE, EDGE), pl.ds(FRAMES, EDGE)
        before, after = pl.ds(0, EDGE), pl.ds(FRAMES + EDGE, EDGE)
        return (
            remote(buf.at[:, first], buf.at[:, after], halo_send, halo_recv.at[number], torus.beside(-1)),
            remote(buf.at[:, last], buf.at[:, before], halo_send, halo_recv.at[number + 1], torus.beside(1)),
        )

    def halo_end(copies, buf):
        inside = (
            jnp.where(seq < 31, 1.0, 0.0).astype(F32),
            jnp.where(seq > 0, 1.0, 0.0).astype(F32),
        )
        for copy, keep, rows in zip(copies, inside, (pl.ds(FRAMES + EDGE, EDGE), pl.ds(0, EDGE))):
            copy.wait_recv()
            buf[:, rows, :] = buf[:, rows, :] * keep

    normalize(0)
    wv_load.wait()
    wg_load.wait()
    gate(0)
    normalize(2)
    gate(2)
    h_halo = halo(hb, 0)
    for copy in h_halo:
        copy.start()
    normalize(1)
    gate(1)

    def near(buf, j, row):
        return buf[j, pl.ds(row, 8), :]

    def convolve(buf, c, tap_at, beside=None):
        def pair(p, _):
            if beside is not None:
                beside(c, p)
            for half in range(2):
                j = 2 * p + half
                for b in range(ROWS // BLOCK):
                    first = ROWS * c + BLOCK * b
                    totals = [None] * (BLOCK // 8)
                    for k in range(TAPS):
                        tap = tap_wide[j, tap_at(k)]
                        for i in range(BLOCK // 8):
                            term = near(buf, j, first + (EDGE - REACH + k + 8 * i)) * tap
                            totals[i] = term if k == 0 else totals[i] + term
                    for i in range(BLOCK // 8):
                        cb[j, pl.ds(first + 8 * i, 8), :] = totals[i]
            return 0

        lax.fori_loop(0, 3, pair, 0)

    def wide(p):
        return pl.ds(pl.multiple_of(256 * p, 256), 256)

    def slope_part(c, p):
        ds[chunk(c), wide(p)] = dot(uf[0, chunk(c), :], wo[0, wide(p), :], ((1,), (1,))) + dot(
            uf[1, chunk(c), :], wo[1, wide(p), :], ((1,), (1,))
        )

    def output_part(c, p):
        part_out[0, chunk(c), wide(p)] = jnp.dot(
            sw[chunk(c), :], wo[other, :, wide(p)], preferred_element_type=F32
        ).astype(BF16)
        po[chunk(c), wide(p)] = jnp.dot(sw[chunk(c), :], wo[me, :, wide(p)], preferred_element_type=F32)

    lane = lax.broadcasted_iota(jnp.int32, (GROUP, 128), 1)

    def stat_copy(number, c):
        at = 3 * number + c
        return remote(
            stat_out.at[number, chunk(c)], stat_in.at[number, chunk(c)], stat_send, stat_recv.at[at], partner
        )

    def put_stats(number, rows, first, second):
        stat_out[number, rows, :] = jnp.where(lane < 64, first, second)

    def get_stats(number, rows):
        total = (stat_out[number, rows, :] + stat_in[number, rows, :]) * (1.0 / WIDTH)
        return total[:, 0:1], total[:, 64:65]

    def conv_stats(c):
        def body(first):
            rows = pl.ds(first, GROUP)
            strips = [cb[j, rows, :] for j in range(6)]
            total, square = strips[0], strips[0] * strips[0]
            for strip in strips[1:]:
                total, square = total + strip, square + strip * strip
            put_stats(0, rows, jnp.sum(total, -1, keepdims=True), jnp.sum(square, -1, keepdims=True))

        groups(c, body)
        stat_copy(0, c).start()

    u_load.wait()
    u_share.wait_recv()
    for load in wo_loads:
        load.wait()
    convolve(hb, 1, lambda k: k, slope_part)
    conv_stats(1)
    halo_end(h_halo, hb)
    for c in (0, 2):
        convolve(hb, c, lambda k: k, slope_part)
        conv_stats(c)

    def store_small(n):
        source, target = ((value_grad, value_out), (gate_grad, gate_out), (out_grad, outer_out), (taps_grad, taps_out))[n]
        store = pltpu.make_async_copy(source, target, store_sem.at[2 + n])
        store.start()
        return store

    def activate(c):
        stat_copy(0, c).wait_recv()

        def body(first):
            rows = pl.ds(first, GROUP)
            mean, square = get_stats(0, rows)
            scale = lax.rsqrt(square - mean * mean + epsilon)
            rstd2[rows, :] = jnp.broadcast_to(scale, (GROUP, 128))
            total = cross = None
            for j in range(6):
                columns = slice(128 * j, 128 * j + 128)
                zhat = (cb[j, rows, :] - mean) * scale
                s = sigmoid(zhat)
                cb[j, rows, :] = zhat
                swish = zhat * s
                sw[rows, columns] = swish.astype(BF16)
                slope = ds[rows, columns] * (s + swish * (1.0 - s))
                ds[rows, columns] = slope
                total = slope if total is None else total + slope
                cross = slope * zhat if cross is None else cross + slope * zhat
            put_stats(1, rows, jnp.sum(total, -1, keepdims=True), jnp.sum(cross, -1, keepdims=True))

        groups(c, body)
        stat_copy(1, c).start()

    for c in (0, 2, 1):
        activate(c)

    def part_copy(number, c):
        at = 3 * number + c
        return remote(
            part_out.at[number, chunk(c)], part_in.at[number, chunk(c)], part_send, part_recv.at[at], partner
        )

    finals = (value_grad, gate_grad, out_grad)
    scatters = [
        [Scatter(torus, g, color, grads, landed, sums, finals, send, recv) for color in range(3)]
        for g in range(GRADS)
    ]

    def weight_grad(g, rows_of, right, n):
        for m in range(4):
            term = dot(rows_of(m), right[:, 256 * n : 256 * n + 256], ((0,), (0,)))
            for half in range(2):
                grads[g, 2 * n + half, m // 2, 2 * (m % 2) : 2 * (m % 2) + 2] = (
                    term[:, 128 * half : 128 * half + 128].reshape(2, 4, 2, 24, 128).astype(BF16)
                )
        scatters[g][n].begin(0)

    def conv_slope(c):
        stat_copy(1, c).wait_recv()

        def body(first):
            rows = pl.ds(first, GROUP)
            mean, cross = get_stats(1, rows)
            scale = rstd2[rows, :]
            for j in range(6):
                slope = scale * (ds[rows, 128 * j : 128 * j + 128] - mean - cb[j, rows, :] * cross)
                db[j, pl.ds(pl.multiple_of(first + EDGE, GROUP), GROUP), :] = slope.astype(BF16).astype(F32)

        groups(c, body)

    conv_slope(0)
    conv_slope(2)
    d_halo = halo(db, 2)
    for copy in d_halo:
        copy.start()
    conv_slope(1)
    for n in range(3):
        weight_grad(2, lambda m: uf[m // 2, :, 384 * (m % 2) : 384 * (m % 2) + 384], sw, n)

    def tap_terms(j):
        def block(b, totals):
            first = pl.multiple_of(BLOCK * b, BLOCK)
            slopes = [near(db, j, pl.multiple_of(first + (EDGE + 8 * i), 8)) for i in range(BLOCK // 8)]
            totals = list(totals)
            for m in range(BLOCK - 8 + TAPS):
                shifted = near(hb, j, first + (EDGE - REACH + m))
                for i in range(BLOCK // 8):
                    if 0 <= m - 8 * i < TAPS:
                        totals[m - 8 * i] = totals[m - 8 * i] + shifted * slopes[i]
            return tuple(totals)

        zeros = tuple(jnp.zeros((8, 128), F32) for _ in range(TAPS))
        totals = lax.fori_loop(0, FRAMES // BLOCK, block, zeros)
        for k in range(TAPS):
            tap_acc[j, k, :] = jnp.sum(totals[k], 0)
        tap_acc[j, TAPS, :] = jnp.zeros((128,), F32)

    tap_sums = [TapSum(torus, color, slots, tap_send, tap_recv) for color in range(3)]

    def tap_color(color):
        tap_sums[color].begin(0, tap_acc[2 * color : 2 * color + 2])

    def relay(g, colors=(0, 1, 2)):
        for color in colors:
            scatters[g][color].relay()

    def finish(g, phase, colors=(0, 1, 2)):
        for color in colors:
            scatters[g][color].finish(phase)

    def tap_step(phase, color):
        total = tap_sums[color].finish(phase)
        if phase < 2:
            tap_sums[color].begin(phase + 1, total)
        else:
            for half in range(2):
                j = 2 * color + half
                taps_grad[:, 128 * j : 128 * j + 128] = total[half, 0:TAPS, :]

    def gate_slopes(c):
        def body(first):
            rows = pl.ds(first, GROUP)
            valid = valid_rows(first, GROUP)
            for j in range(6):
                columns = slice(128 * j, 128 * j + 128)
                sigma = sg[rows, columns]
                slope = cb[j, rows, :] * valid * sigma
                dv[rows, columns] = slope.astype(BF16)
                dg[rows, columns] = (slope * vb[rows, columns] * (1.0 - sigma)).astype(BF16)

        groups(c, body)

    convolve(db, 1, lambda k: TAPS - 1 - k, output_part)
    part_copy(0, 1).start()
    gate_slopes(1)
    halo_end(d_halo, db)
    convolve(db, 0, lambda k: TAPS - 1 - k, output_part)
    part_copy(0, 0).start()
    gate_slopes(0)
    relay(2, (0,))
    convolve(db, 2, lambda k: TAPS - 1 - k, output_part)
    part_copy(0, 2).start()
    gate_slopes(2)

    for n in range(3):
        weight_grad(0, lambda m: nb[:, 384 * m : 384 * m + 384], dv, n)
    relay(2, (1, 2))
    for n in range(3):
        weight_grad(1, lambda m: nb[:, 384 * m : 384 * m + 384], dg, n)

    def features(c, n, half):
        rows = pl.ds(pl.multiple_of(half * HALF + 256 * n, 256), 256)
        return dot(dv[chunk(c), :], wv[rows, :], ((1,), (1,))) + dot(dg[chunk(c), :], wg[rows, :], ((1,), (1,)))

    def features_over(c):
        for n in range(3):
            part_out[1, chunk(c), 256 * n : 256 * n + 256] = features(c, n, other).astype(BF16)
        part_copy(1, c).start()

    def features_here(c):
        for n in range(3):
            vb[chunk(c), 256 * n : 256 * n + 256] = features(c, n, me)

    def output_rows(c):
        part_copy(0, c).wait_recv()

        def body(first):
            rows = pl.ds(first, GROUP)
            total = xf[me, rows, :].astype(F32) + (po[rows, :] + part_in[0, rows, :].astype(F32))
            xf[me, rows, :] = total.astype(BF16)

        groups(c, body)
        store = pltpu.make_async_copy(xf.at[me, chunk(c)], out.at[chunk(c)], store_sem.at[0])
        store.start()

    def feature_stats(c):
        part_copy(1, c).wait_recv()

        def body(first):
            rows = pl.ds(first, GROUP)
            slope = vb[rows, :] + part_in[1, rows, :].astype(F32)
            vb[rows, :] = slope
            unit = nb[rows, pl.ds(pl.multiple_of(me * HALF, HALF), HALF)].astype(F32)
            put_stats(2, rows, jnp.sum(slope, -1, keepdims=True), jnp.sum(slope * unit, -1, keepdims=True))

        groups(c, body)
        stat_copy(2, c).start()

    def input_rows(c):
        stat_copy(2, c).wait_recv()

        def body(first):
            rows = pl.ds(first, GROUP)
            mean, cross = get_stats(2, rows)
            scale = rstd1[rows, 0:1]
            unit = nb[rows, pl.ds(pl.multiple_of(me * HALF, HALF), HALF)].astype(F32)
            total = uf[me, rows, :].astype(F32) + scale * (vb[rows, :] - mean - unit * cross)
            uf[me, rows, :] = total.astype(BF16)

        groups(c, body)
        store = pltpu.make_async_copy(uf.at[me, chunk(c)], grad_in.at[chunk(c)], store_sem.at[1])
        store.start()

    tap_terms(0)
    tap_terms(1)
    tap_color(0)
    relay(0, (0,))
    tap_terms(2)
    relay(0, (1,))
    finish(2, 0, (0,))
    tap_terms(3)
    tap_color(1)
    finish(2, 0, (1,))
    tap_terms(4)
    relay(0, (2,))
    finish(2, 0, (2,))
    tap_terms(5)
    tap_color(2)
    features_over(0)
    relay(1, (0,))
    tap_step(0, 0)
    features_over(1)
    relay(1, (1,))
    features_over(2)
    relay(1, (2,))
    finish(0, 0, (0,))
    tap_step(0, 1)
    features_here(0)
    finish(0, 0, (1,))
    tap_step(1, 0)
    features_here(1)
    finish(0, 0, (2,))
    finish(1, 0, (0,))
    finish(2, 1)
    features_here(2)
    finish(1, 0, (1,))
    tap_step(0, 2)
    for c in range(CHUNKS):
        feature_stats(c)
    finish(1, 0, (2,))
    tap_step(1, 1)
    finish(0, 1)
    for c in range(CHUNKS):
        output_rows(c)
    tap_step(2, 0)
    for c in range(CHUNKS):
        input_rows(c)
    finish(2, 2)
    stores = [store_small(2)]
    finish(1, 1)
    tap_step(1, 2)
    tap_step(2, 1)
    finish(0, 2)
    stores.append(store_small(0))
    finish(1, 2)
    stores.append(store_small(1))
    tap_step(2, 2)
    stores.append(store_small(3))

    for color in range(3):
        for phase in range(3):
            wait_bytes(torus, landed[color][phase], send.at[color * 3 + phase], sent=True)
    wait_bytes(torus, slots.at[:, :, 0:3], tap_send, sent=True)
    wait_bytes(torus, xf.at[me], x_send, sent=True)
    wait_bytes(torus, uf.at[me], u_send, sent=True)
    wait_bytes(torus, hb.at[:, 0 : 4 * EDGE], halo_send, sent=True)
    wait_bytes(torus, stat_out, stat_send, sent=True)
    wait_bytes(torus, part_out, part_send, sent=True)
    pltpu.make_async_copy(xf.at[me], out, store_sem.at[0]).wait()
    pltpu.make_async_copy(uf.at[me], grad_in, store_sem.at[1]).wait()
    for store in stores:
        store.wait()


def place_kernel(*refs):
    sources, targets, held, (load, store) = refs[:6], refs[6:12], refs[12:18], refs[18:]
    parts = [(n, slice(None)) for n in range(2, 6)]
    parts += [(n, pl.ds(ROWS * c, ROWS)) for n in range(2) for c in range(CHUNKS)]
    pairs = [
        (
            pltpu.make_async_copy(sources[n].at[rows], held[n].at[rows], load.at[at]),
            pltpu.make_async_copy(held[n].at[rows], targets[n].at[rows], store.at[at]),
        )
        for at, (n, rows) in enumerate(parts)
    ]
    for first, _ in pairs:
        first.start()
    for first, second in pairs:
        first.wait()
        second.start()
    for _, second in pairs:
        second.wait()


def scratch_shapes():
    vmem, dma = pltpu.VMEM, pltpu.SemaphoreType.DMA
    shapes = [vmem((GRADS, 2, 3) + dims + (24, 128), BF16) for order in ORDERS for dims in LEFT[order]]
    shapes += [vmem((GRADS, 2) + dims + (24, 128), BF16) for order in ORDERS for dims in LEFT[order][:2]]
    shapes += [vmem((3, 3, 4, 2, 32, 128), BF16), dma((9,)), dma((GRADS * 3 * 4,)), dma(()), dma((9,))]
    square, padded = (FRAMES, HALF), (6, FRAMES + 2 * EDGE, 128)
    shapes += [
        vmem((GRADS, 6, 2, 4, 4, 2, 24, 128), BF16),
        vmem((2,) + square, BF16),
        vmem((2,) + square, BF16),
        vmem((WIDTH, HALF), BF16),
        vmem((WIDTH, HALF), BF16),
        vmem((2,) + square, BF16),
        vmem((FRAMES, WIDTH), BF16),
        vmem((FRAMES, 128), F32),
        vmem(square, F32),
        vmem(square, F32),
        vmem(padded, F32),
        vmem(padded, F32),
        vmem((6, FRAMES, 128), F32),
        vmem(square, BF16),
        vmem(square, F32),
        vmem((FRAMES, 128), F32),
        vmem((3, FRAMES, 128), F32),
        vmem((3, FRAMES, 128), F32),
        vmem(square, BF16),
        vmem(square, BF16),
        vmem(square, F32),
        vmem((2,) + square, BF16),
        vmem((2,) + square, BF16),
        vmem((TAPS, HALF), BF16),
        vmem((1, 1), jnp.int32),
        vmem((6, TAPS, 8, 128), F32),
        vmem((6, TAPS + 1, 128), F32),
        vmem((24, HALF), F32), vmem((24, HALF), F32), vmem((24, HALF), F32), vmem((TAPS, HALF), F32),
        dma((10,)), dma(()), dma((3,)), dma(()), dma(()), dma(()), dma((4,)),
        dma(()), dma((9,)), dma(()), dma((6,)), dma((6,)),
    ]
    return shapes


def shards(inputs, lengths, cotangent, w_value, w_gate, kernel_taps, w_out):
    here = pl.BlockSpec(memory_space=pl.ANY)
    rows = jax.ShapeDtypeStruct((FRAMES, HALF), BF16)
    block = jax.ShapeDtypeStruct((24, HALF), F32)
    results = (rows, rows, block, block, jax.ShapeDtypeStruct((TAPS, HALF), F32), block)
    output, input_gradient, value_grad, gate_grad, kernel_grad, out_grad = pl.pallas_call(
        kernel,
        out_shape=results,
        in_specs=[here] * 7,
        out_specs=(here,) * 6,
        scratch_shapes=scratch_shapes(),
        compiler_params=pltpu.CompilerParams(
            collective_id=0, has_side_effects=True, vmem_limit_bytes=67043328
        ),
    )(lengths.reshape(1, 1), inputs[0], cotangent[0], w_value, w_gate, kernel_taps, w_out)
    output, input_gradient, value_grad, gate_grad, kernel_grad, out_grad = pl.pallas_call(
        place_kernel,
        out_shape=results,
        in_specs=[here] * 6,
        out_specs=(here,) * 6,
        scratch_shapes=[pltpu.VMEM(result.shape, result.dtype) for result in results]
        + [pltpu.SemaphoreType.DMA((10,)), pltpu.SemaphoreType.DMA((10,))],
    )(output, input_gradient, value_grad, gate_grad, kernel_grad, out_grad)
    return (output[None], input_gradient[None], value_grad, gate_grad, kernel_grad, out_grad.T)


def solution(mesh):
    return jax.shard_map(
        shards,
        mesh=mesh,
        in_specs=(
            P("dp", "seq", "tensor"),
            P("dp"),
            P("dp", "seq", "tensor"),
            P(None, "tensor"),
            P(None, "tensor"),
            P(None, "tensor"),
            P("tensor", None),
        ),
        out_specs=(
            P("dp", "seq", "tensor"),
            P("dp", "seq", "tensor"),
            P(("seq", "dp"), "tensor"),
            P(("seq", "dp"), "tensor"),
            P(None, "tensor"),
            P("tensor", ("seq", "dp")),
        ),
        check_vma=False,
    )
```

time: 96.1 us -> 78.5 us (0.82)
  Pallas kernels: 94.4 us -> 76.9 us
    pallas_call x2, Pallas kernels: 94.4 us -> 76.9 us  [the longest x1 74.2 us: shards(): pl.pallas_call(kernel, out_shape=results, in_specs=[here] * 7, out_specs=...]
where the time goes in v2:
time: 78.5 us; the launch traced here: 78.4 us
  Pallas kernels  76.9 us (98%)
  between operations  1.45 us (2%)
    pallas_call x1, Pallas kernels, shards(): pl.pallas_call(kernel, out_shape=results, in_specs=[here] * 7, out_specs=...  74.2 us
    pallas_call x1, Pallas kernels, shards(): pl.pallas_call(place_kernel, out_shape=results, in_specs=[here] * 6, out_...  2.73 us

profile of v2, /device:TPU:0, one launch (start us, length us, event | category | flops | bytes accessed | tf_op | source)
XLA Modules:
  0.0 78.4 jit_solution(1001767444199950410)
XLA Ops:
  1.3 74.2 %shard_map.118 = (bf16[768,768]{1,0:T(8,128)(2,1)}, bf16[768,768]{1,0:T(8,128)(2,1)}, f32[24,768]{1,0:T(8,128)}, f32[24,768]{1,0:T(8,128)}, f32[31,768]{1,0:T(8,128)}, /*index=5*/f32[24,768]{1,0:T(8,128)}) custom-call(s32[1,1]{1,0:T(1,128)} %bitcast.6.lengths, bf16[768,768]{1,0:T(8,128)(2,1)} %bitcast.7, bf16[768,768]{1,0:T(8,128)(2,1)} %bitcast.8, ...), custom_call_target="tpu_custom_call" | custom-call | tf_op jit(solution)/shard_map/pallas_call | solution.py:721
  75.5 2.7 %shard_map.119 = (bf16[768,768]{1,0:T(8,128)(2,1)}, bf16[768,768]{1,0:T(8,128)(2,1)}, f32[24,768]{1,0:T(8,128)}, f32[24,768]{1,0:T(8,128)}, f32[31,768]{1,0:T(8,128)}, /*index=5*/f32[24,768]{1,0:T(8,128)}) custom-call(bf16[768,768]{1,0:T(8,128)(2,1)} %get-tuple-element.18.refs_0_, bf16[768,768]{1,0:T(8,128)(2,1)} %get-tuple-element.19.refs_1_, ...), custom_call_target="tpu_custom_call" | custom-call | tf_op jit(solution)/shard_map/pallas_call | solution.py:731

commit v3 on v2

--- a/solution.py
+++ b/solution.py
@@ -100,10 +100,13 @@
         for half, way in ((0, 1), (1, -1)):
             if phase == 0:
                 self.send(0, half, 0, self.held(0, half, 2), way).start()
-                self.send(0, half, 1, self.held(0, half, -way), -way).start()
             else:
                 for which, by in enumerate((2, -way, way)):
                     self.send(phase, half, which, self.held(phase, half, by), by).start()
+
+    def straight(self):
+        for half, way in ((0, 1), (1, -1)):
+            self.send(0, half, 1, self.held(0, half, -way), -way).start()
 
     def relay(self):
         wait_bytes(self.torus, self.landed[0].at[self.grad, :, 0], self.arrived(0, 0))
@@ -216,15 +219,15 @@
         x_load(c).start()
     tap_load.start()
     length_load.start()
+    greet(torus)
+    for c in (0, 2, 1):
+        x_share(c).start()
     wv_load.start()
     wg_load.start()
     u_load.start()
+    u_share.start()
     for load in wo_loads:
         load.start()
-    greet(torus)
-    for c in (0, 2, 1):
-        x_share(c).start()
-    u_share.start()
 
     tap_load.wait()
     length_load.wait()
@@ -453,9 +456,12 @@
     d_halo = halo(db, 2)
     for copy in d_halo:
         copy.start()
-    conv_slope(1)
     for n in range(3):
         weight_grad(2, lambda m: uf[m // 2, :, 384 * (m % 2) : 384 * (m % 2) + 384], sw, n)
+    for color in range(3):
+        scatters[2][color].straight()
+
+    conv_slope(1)
 
     def tap_terms(j):
         def block(b, totals):
@@ -480,6 +486,10 @@
     def tap_color(color):
         tap_sums[color].begin(0, tap_acc[2 * color : 2 * color + 2])
 
+    def straight(g):
+        for color in range(3):
+            scatters[g][color].straight()
+
     def relay(g, colors=(0, 1, 2)):
         for color in colors:
             scatters[g][color].relay()
@@ -517,14 +527,13 @@
     convolve(db, 0, lambda k: TAPS - 1 - k, output_part)
     part_copy(0, 0).start()
     gate_slopes(0)
-    relay(2, (0,))
+    relay(2)
     convolve(db, 2, lambda k: TAPS - 1 - k, output_part)
     part_copy(0, 2).start()
     gate_slopes(2)
 
     for n in range(3):
         weight_grad(0, lambda m: nb[:, 384 * m : 384 * m + 384], dv, n)
-    relay(2, (1, 2))
     for n in range(3):
         weight_grad(1, lambda m: nb[:, 384 * m : 384 * m + 384], dg, n)
 
@@ -581,59 +590,59 @@
         store = pltpu.make_async_copy(uf.at[me, chunk(c)], grad_in.at[chunk(c)], store_sem.at[1])
         store.start()
 
+    straight(0)
     tap_terms(0)
+    relay(0, (0,))
     tap_terms(1)
     tap_color(0)
-    relay(0, (0,))
+    relay(0, (1, 2))
+    straight(1)
     tap_terms(2)
-    relay(0, (1,))
-    finish(2, 0, (0,))
+    finish(2, 0)
     tap_terms(3)
     tap_color(1)
-    finish(2, 0, (1,))
+    relay(1, (0,))
     tap_terms(4)
-    relay(0, (2,))
-    finish(2, 0, (2,))
+    relay(1, (1, 2))
     tap_terms(5)
     tap_color(2)
+    tap_step(0, 0)
     features_over(0)
-    relay(1, (0,))
-    tap_step(0, 0)
+    finish(0, 0, (0,))
     features_over(1)
-    relay(1, (1,))
+    finish(0, 0, (1, 2))
     features_over(2)
-    relay(1, (2,))
-    finish(0, 0, (0,))
+    finish(1, 0, (0,))
+    features_here(0)
+    finish(1, 0, (1,))
     tap_step(0, 1)
-    features_here(0)
-    finish(0, 0, (1,))
+    features_here(1)
+    finish(1, 0, (2,))
+    tap_step(0, 2)
+    features_here(2)
     tap_step(1, 0)
-    features_here(1)
-    finish(0, 0, (2,))
-    finish(1, 0, (0,))
-    finish(2, 1)
-    features_here(2)
-    finish(1, 0, (1,))
-    tap_step(0, 2)
     for c in range(CHUNKS):
         feature_stats(c)
-    finish(1, 0, (2,))
-    tap_step(1, 1)
-    finish(0, 1)
+    finish(0, 1, (0,))
     for c in range(CHUNKS):
         output_rows(c)
-    tap_step(2, 0)
+    finish(0, 1, (1, 2))
+    finish(2, 1)
     for c in range(CHUNKS):
         input_rows(c)
+    finish(1, 1, (0,))
+    finish(1, 1, (1,))
+    tap_step(1, 1)
+    finish(1, 1, (2,))
+    tap_step(1, 2)
+    finish(0, 2)
+    stores = [store_small(0)]
+    tap_step(2, 0)
     finish(2, 2)
-    stores = [store_small(2)]
-    finish(1, 1)
-    tap_step(1, 2)
-    tap_step(2, 1)
-    finish(0, 2)
-    stores.append(store_small(0))
+    stores.append(store_small(2))
     finish(1, 2)
     stores.append(store_small(1))
+    tap_step(2, 1)
     tap_step(2, 2)
     stores.append(store_small(3))
 

time: 78.5 us -> 77.6 us (0.989)
  Pallas kernels: 76.9 us -> 75.8 us
    pallas_call x1, Pallas kernels: 74.2 us -> 73.1 us  [shards(): pl.pallas_call(kernel, out_shape=results, in_specs=[here] * 7, out_specs=...]
where the time goes in v3:
time: 77.6 us; the launch traced here: 77.3 us
  Pallas kernels  75.8 us (98%)
  between operations  1.45 us (2%)
    pallas_call x1, Pallas kernels, shards(): pl.pallas_call(kernel, out_shape=results, in_specs=[here] * 7, out_specs=...  73.1 us
    pallas_call x1, Pallas kernels, shards(): pl.pallas_call(place_kernel, out_shape=results, in_specs=[here] * 6, out_...  2.73 us

profile of v3, /device:TPU:0, one launch (start us, length us, event | category | flops | bytes accessed | tf_op | source)
XLA Modules:
  0.0 77.3 jit_solution(6318218392205837976)
XLA Ops:
  1.3 73.1 %shard_map.118 = (bf16[768,768]{1,0:T(8,128)(2,1)}, bf16[768,768]{1,0:T(8,128)(2,1)}, f32[24,768]{1,0:T(8,128)}, f32[24,768]{1,0:T(8,128)}, f32[31,768]{1,0:T(8,128)}, /*index=5*/f32[24,768]{1,0:T(8,128)}) custom-call(s32[1,1]{1,0:T(1,128)} %bitcast.6.lengths, bf16[768,768]{1,0:T(8,128)(2,1)} %bitcast.7, bf16[768,768]{1,0:T(8,128)(2,1)} %bitcast.8, ...), custom_call_target="tpu_custom_call" | custom-call | tf_op jit(solution)/shard_map/pallas_call | solution.py:730
  74.4 2.7 %shard_map.119 = (bf16[768,768]{1,0:T(8,128)(2,1)}, bf16[768,768]{1,0:T(8,128)(2,1)}, f32[24,768]{1,0:T(8,128)}, f32[24,768]{1,0:T(8,128)}, f32[31,768]{1,0:T(8,128)}, /*index=5*/f32[24,768]{1,0:T(8,128)}) custom-call(bf16[768,768]{1,0:T(8,128)(2,1)} %get-tuple-element.18.refs_0_, bf16[768,768]{1,0:T(8,128)(2,1)} %get-tuple-element.19.refs_1_, ...), custom_call_target="tpu_custom_call" | custom-call | tf_op jit(solution)/shard_map/pallas_call | solution.py:740
